TPU v7x, 32 devices: a whole 2x2x4 slice. The times are simulated.
32 devices in a mesh: trial: 8 (over z, y), tensor: 4 (over x, core).
Axes of the slice: x: 2, y: 2, z: 4, core: 2. Of those that a mesh axis runs over, the one named last changes fastest.
Arguments:
- stored_attention: bfloat16 [8, 1024, 8192], P('trial', None, 'tensor'), may hold values from -6 to 6
- output_gradient: bfloat16 [8, 1024, 8192], P('trial', 'tensor'), may hold values from -6 to 6
- output_weight: bfloat16 [8192, 8192], P('tensor', 'trial'), may hold values from -0.0625 to 0.0625
- down_adapter: bfloat16 [8, 8192, 128], P('trial', 'tensor'), may hold values from -0.0625 to 0.0625
- up_adapter: bfloat16 [8, 128, 8192], P('trial'), may hold values from -0.0625 to 0.0625
- lengths: int32 [8], P('trial'), may hold values from 128 to 1024, as said below
- ranks: int32 [8], P('trial'), may hold values from 16 to 128, as said below
Outputs:
- attention_gradient: bfloat16 [8, 1024, 8192], P('trial', None, 'tensor')
- down_gradient: float32 [8, 8192, 128], P('trial', 'tensor')
- up_gradient: float32 [8, 128, 8192], P('trial', None, 'tensor')
Inputs may be any that keep to these rules, and one draw needn't show every extreme that they name: `lengths`: rows at or beyond a trial's count are padding; some trial has all 1024 rows live. `ranks`: each rank is a multiple of 16; some trial has rank 128 and some has 16.
All inputs are finite; a program needn't handle non-finite values.
Results may differ from a plain program's by a relative error of at most 0.0034.
Values may be sent and summed in bfloat16 or wider, within the bound.
A program may use at most 128 MiB of HBM per device.

v0:
```python
import jax
import jax.numpy as jnp
from jax import lax
from jax.sharding import PartitionSpec as P

adapter_alpha = 32.0


def row_product(left, right):
    return jnp.einsum("tk,hk->th", left, right, preferred_element_type=jnp.float32)


def body(
    stored_attention, output_gradient, output_weight, down_adapter, up_adapter, lengths, ranks
):
    attention_rows = stored_attention[0]
    gradient_rows = output_gradient[0]
    down_piece = down_adapter[0]
    up_complete = up_adapter[0]
    length = lengths[0]
    adapter_rank = ranks[0]
    token_rows = attention_rows.shape[0]
    head_cols = attention_rows.shape[1]
    shard_rows = gradient_rows.shape[0]
    rank_mask = jnp.arange(up_complete.shape[0]) < adapter_rank
    adapter_scale = adapter_alpha / jnp.sqrt(adapter_rank.astype(jnp.float32))
    a_low = jnp.where(rank_mask[None, :], down_piece, jnp.zeros_like(down_piece))
    b_low = jnp.where(rank_mask[:, None], up_complete, jnp.zeros_like(up_complete))
    row_offset = lax.axis_index("tensor") * shard_rows
    live_rows = row_offset + jnp.arange(shard_rows) < length
    gradient_rows = jnp.where(live_rows[:, None], gradient_rows, jnp.zeros_like(gradient_rows))
    u_part = jnp.einsum(
        "td,rd->tr", gradient_rows, b_low, preferred_element_type=jnp.float32
    ).astype(jnp.bfloat16)
    v_partial = jnp.dot(attention_rows, a_low, preferred_element_type=jnp.float32)
    lowrank_right = lax.psum(v_partial, "tensor").astype(jnp.bfloat16)
    col_start = lax.axis_index("tensor") * head_cols
    rows_all, u_all = (
        lax.all_gather(gradient_rows, "tensor", axis=0, tiled=True),
        lax.all_gather(u_part, "tensor", axis=0, tiled=True),
    )
    dense_piece = row_product(rows_all, lax.all_gather(output_weight, "trial", axis=1, tiled=True))
    lowrank_piece = jnp.einsum("tr,hr->th", u_all, a_low, preferred_element_type=jnp.float32)
    attention_gradient = (dense_piece + adapter_scale * lowrank_piece).astype(jnp.bfloat16)
    down_total = jnp.einsum("th,tr->hr", attention_rows, u_all, preferred_element_type=jnp.float32)
    own_cols = lax.dynamic_slice_in_dim(rows_all, col_start, head_cols, 1)
    up_total = jnp.einsum("tr,th->rh", lowrank_right, own_cols, preferred_element_type=jnp.float32)
    down_gradient = adapter_scale * down_total / float(token_rows)
    up_gradient = adapter_scale * up_total / float(token_rows)
    return (attention_gradient[None], down_gradient[None], up_gradient[None])


def solution(mesh):
    placed = (
        P("trial", None, "tensor"),
        P("trial", "tensor", None),
        P("tensor", "trial"),
        P("trial", "tensor", None),
        P("trial", None, None),
        P("trial"),
        P("trial"),
    )
    return jax.shard_map(
        body,
        mesh=mesh,
        in_specs=placed,
        out_specs=(
            P("trial", None, "tensor"),
            P("trial", "tensor", None),
            P("trial", None, "tensor"),
        ),
        check_vma=False,
    )
```

profile of v0, /device:TPU:0, one launch (start us, length us, event | category | flops | bytes accessed | tf_op | source)
XLA Modules:
  0.0 825.9 jit_solution(16108703871894892472)
XLA Ops:
  7.2 0.0 all-gather.3.cloned.1.call-start
  7.9 4.5 bitcast_select_fusion
  12.4 0.0 all-gather.3.cloned.1.call-update
  12.4 0.0 all-gather.5.cloned.1.call-start
  12.5 0.7 all-gather.5.cloned.1.call-update
  13.9 0.0 copy-start
  13.9 4.3 fusion.36
  18.2 0.0 copy-start.1
  18.3 7.3 all_gather.11
  25.6 0.0 copy-done
  25.6 0.7 fusion.20
  26.3 1.3 copy.10
  27.6 0.0 copy-done.1
  27.6 4.3 fusion.33
  32.0 26.7 %all-reduce.1 = bf16[1024,128]{0,1:T(8,128)(2,1)S(1)} all-reduce(f32[1024,128]{0,1:T(8,128)S(1)} %fusion.33), channel_id=1, replica_groups=mesh['trial'=8,'tensor'=4] {'tensor'}, use_global_device_ids=true, to_apply=%region_0.1 | all-reduce | flops 131072 | bytes 786432 | tf_op jit(solution)/shard_map/psum | solution.py:36
  58.7 71.0 %all-gather.3.cloned.1.call-done = bf16[1024,8192]{1,0:T(8,128)(2,1)} async-done(((bf16[256,8192]{1,0:T(8,128)(2,1)}), bf16[1024,8192]{1,0:T(8,128)(2,1)}) %all-gather.3.cloned.1.call-update) | async-done | bytes 16777232 | tf_op jit(solution)/shard_map/all_gather | solution.py:39
  129.6 3.9 fusion.26
  133.5 635.4 %all-gather.5.cloned.1.call-done = bf16[2048,8192]{1,0:T(8,128)(2,1)} async-done(((bf16[2048,1024]{1,0:T(8,128)(2,1)}), bf16[2048,8192]{1,0:T(8,128)(2,1)}) %all-gather.5.cloned.1.call-update) | async-done | bytes 33554448 | tf_op jit(solution)/shard_map/all_gather | solution.py:42
  769.0 43.4 %fusion.53 = f32[1024,2048]{1,0:T(8,128)} fusion(bf16[1024,8192]{1,0:T(8,128)(2,1)} %all-gather.3.cloned.1.call-done, bf16[2048,8192]{1,0:T(8,128)(2,1)} %all-gather.5.cloned.1.call-done), kind=kOutput, calls=%fused_computation.40 | convolution fusion | flops 34359738368 | bytes 58720256 | tf_op jit(solution)/shard_map/tk,hk->th/dot_general | solution.py:10
  812.4 6.6 fusion.10
  (2 shorter events, 0.0 us)
Async XLA Ops:
  7.2 122.5 %all-gather.3.cloned.1.call-start = ((), (), s32[]{:S(2)}) async-start(), calls=%async_computation | async-start | bytes 20971520 | tf_op jit(solution)/shard_map/all_gather | solution.py:39
  12.4 756.5 %all-gather.5.cloned.1.call-start = ((), (), s32[]{:S(2)}) async-start(), calls=%async_computation.1 | async-start | bytes 37748736 | tf_op jit(solution)/shard_map/all_gather | solution.py:42
  13.9 11.7 %copy-start = (bf16[1,1024,2048]{2,1,0:T(8,128)(2,1)S(1)}, bf16[1,1024,2048]{2,1,0:T(8,128)(2,1)}, u32[]{:S(2)}) copy-start(bf16[1,1024,2048]{2,1,0:T(8,128)(2,1)} %param.7) | copy-start | bytes 12582916
  18.2 9.4 %copy-start.1 = (bf16[1,2048,128]{2,1,0:T(8,128)(2,1)S(1)}, bf16[1,2048,128]{2,1,0:T(8,128)(2,1)}, u32[]{:S(2)}) copy-start(bf16[1,2048,128]{2,1,0:T(8,128)(2,1)} %param.10) | copy-start | bytes 1572868
Sparse Core Ops, SparseCore 0:
  12.6 117.0 all-gather.2
  131.2 637.7 all-gather.4
where the time goes:
time: 826 us
  waiting for transfers between devices  707 us (86%)
  matrix products  63.4 us (8%)
  blocking collectives  34 us (4%)
  between operations  15.4 us (2%)
    all_gather x1, waiting for transfers between devices, body(): lax.all_gather(output_weight, 'trial', axis=1, tiled=True)  635 us
    all_gather x1, waiting for transfers between devices, body(): lax.all_gather(gradient_rows, 'tensor', axis=0, tiled=True)  71 us
    dot_general x1, matrix products, row_product(): jnp.einsum('tk,hk->th', left, right, preferred_element_type=jnp.float32)  43.4 us
    psum x1, blocking collectives, body(): lowrank_right = lax.psum(v_partial, 'tensor').astype(jnp.bfloat16)  26.7 us
  transfers between devices with their start and end apart: 2, of which 2 were waited for; matrix products, arithmetic and copies ran while one was open for 2% of the time, Pallas kernels for 0%

commit v1 on v0

--- a/solution.py
+++ b/solution.py
@@ -4,6 +4,27 @@
 from jax.sharding import PartitionSpec as P
 
 adapter_alpha = 32.0
+
+
+def collect(shard, axis, dim):
+    devices, mine, rows = (lax.axis_size(axis), lax.axis_index(axis), shard.shape[dim])
+    ahead = [(i, (i + 1) % devices) for i in range(devices)]
+    backward = [(i, (i - 1) % devices) for i in range(devices)]
+    whole = jnp.zeros((*shard.shape[:dim], devices * rows, *shard.shape[dim + 1 :]), shard.dtype)
+    whole = lax.dynamic_update_slice_in_dim(whole, shard, mine * rows, axis=dim)
+    from_left = from_right = shard
+    half = devices // 2
+    for turn in range(1, half + 1):
+        from_left = lax.ppermute(from_left, axis, ahead)
+        whole = lax.dynamic_update_slice_in_dim(
+            whole, from_left, (mine - turn) % devices * rows, axis=dim
+        )
+        if turn < devices - half:
+            from_right = lax.ppermute(from_right, axis, backward)
+            whole = lax.dynamic_update_slice_in_dim(
+                whole, from_right, (mine + turn) % devices * rows, axis=dim
+            )
+    return whole
 
 
 def row_product(left, right):
@@ -39,7 +60,7 @@
         lax.all_gather(gradient_rows, "tensor", axis=0, tiled=True),
         lax.all_gather(u_part, "tensor", axis=0, tiled=True),
     )
-    dense_piece = row_product(rows_all, lax.all_gather(output_weight, "trial", axis=1, tiled=True))
+    dense_piece = row_product(rows_all, collect(output_weight, "trial", 1))
     lowrank_piece = jnp.einsum("tr,hr->th", u_all, a_low, preferred_element_type=jnp.float32)
     attention_gradient = (dense_piece + adapter_scale * lowrank_piece).astype(jnp.bfloat16)
     down_total = jnp.einsum("th,tr->hr", attention_rows, u_all, preferred_element_type=jnp.float32)

time: 826 us -> 715 us (0.87)
  waiting for transfers between devices: 707 us -> 539 us
  local copies, waits for them, and re-layouts: 1.32 us -> 49.5 us
  starting transfers between devices: 0.08 us -> 19.7 us
  blocking collectives: 34 us -> 23.6 us
    all_gather x1 -> x0, waiting for transfers between devices: 635 us -> none  [body(): lax.all_gather(output_weight, 'trial', axis=1, tiled=True)]
    ppermute x0 -> x7, waiting for transfers between devices: none -> 539 us  [the longest x4 539 us: collect(): from_left = lax.ppermute(from_left, axis, ahead)]
    all_gather x1, waiting for transfers between devices: 71 us -> 0.01 us  [body(): lax.all_gather(gradient_rows, 'tensor', axis=0, tiled=True)]
    dynamic_update_slice x0 -> x8, local copies, waits for them, and re-layouts: none -> 34.5 us  [the longest x4 18.4 us: collect(): lax.dynamic_update_slice_in_dim(whole, from_left, (mine - turn) % devices...]
    ppermute x0 -> x7, starting transfers between devices: none -> 19.7 us  [the longest x4 10.5 us: collect(): from_left = lax.ppermute(from_left, axis, ahead)]
    broadcast_in_dim x0 -> x1, local copies, waits for them, and re-layouts: none -> 11.7 us  [collect(): jnp.zeros((*shard.shape[:dim], devices * rows, *shard.shape[dim + 1:]), s...]
    psum x1, blocking collectives: 26.7 us -> 17.8 us  [body(): lowrank_right = lax.psum(v_partial, 'tensor').astype(jnp.bfloat16)]
  transfers between devices with their start and end apart: 2 -> 8, of which waited for: 2 -> 4; matrix products, arithmetic and copies ran while one was open for 2% -> 8% of each run, Pallas kernels for 0% -> 0%
where the time goes in v1:
time: 715 us; the launch traced here: 714 us
  waiting for transfers between devices  539 us (75%)
  matrix products  62.1 us (9%)
  local copies, waits for them, and re-layouts  49.5 us (7%)
  blocking collectives  23.6 us (3%)
  starting transfers between devices  19.7 us (3%)
  between operations  15.5 us (2%)
    ppermute x4, waiting for transfers between devices, collect(): from_left = lax.ppermute(from_left, axis, ahead)  539 us
    dot_general x1, matrix products, row_product(): jnp.einsum('tk,hk->th', left, right, preferred_element_type=jnp.float32)  45.1 us
    dynamic_update_slice x4, local copies, waits for them, and re-layouts, collect(): lax.dynamic_update_slice_in_dim(whole, from_left, (mine - turn) % devices...  18.4 us
    psum x1, blocking collectives, body(): lowrank_right = lax.psum(v_partial, 'tensor').astype(jnp.bfloat16)  17.8 us
  transfers between devices with their start and end apart: 8, of which 4 were waited for; matrix products, arithmetic and copies ran while one was open for 8% of the time, Pallas kernels for 0%

profile of v1, /device:TPU:0, one launch (start us, length us, event | category | flops | bytes accessed | tf_op | source)
XLA Modules:
  0.0 714.0 jit_solution(16821542163314245398)
XLA Ops:
  7.2 0.0 all-gather.2.cloned.1.call-start
  7.9 4.5 bitcast_select_fusion
  12.4 3.0 collective-permute-start
  15.5 3.1 collective-permute-start.1
  18.6 176.9 %collective-permute-done = bf16[2048,1024]{1,0:T(8,128)(2,1)S(1)} collective-permute-done((bf16[2048,1024]{1,0:T(8,128)(2,1)}, bf16[2048,1024]{1,0:T(8,128)(2,1)S(1)}, u32[]{:S(2)}, u32[]{:S(2)}) %collective-permute-start) | collective-permute-done | bytes 4194336 | tf_op jit(solution)/shard_map/ppermute | solution.py:18
  195.5 2.0 copy-done.2
  197.5 2.4 collective-permute-start.2
  199.9 3.0 collective-permute-start.3
  202.9 175.8 %collective-permute-done.2 = bf16[2048,1024]{1,0:T(8,128)(2,1)} collective-permute-done((bf16[2048,1024]{1,0:T(8,128)(2,1)S(1)}, bf16[2048,1024]{1,0:T(8,128)(2,1)}, u32[]{:S(2)}, u32[]{:S(2)}) %collective-permute-start.2) | collective-permute-done | bytes 4194336 | tf_op jit(solution)/shard_map/ppermute | solution.py:18
  378.7 2.6 collective-permute-start.4
  382.0 3.1 collective-permute-start.5
  385.1 3.7 fusion.33
  388.8 171.1 %collective-permute-done.4 = bf16[2048,1024]{1,0:T(8,128)(2,1)} collective-permute-done((bf16[2048,1024]{1,0:T(8,128)(2,1)}, bf16[2048,1024]{1,0:T(8,128)(2,1)}, u32[]{:S(2)}, u32[]{:S(2)}) %collective-permute-start.4) | collective-permute-done | bytes 4194336 | tf_op jit(solution)/shard_map/ppermute | solution.py:18
  559.9 2.5 collective-permute-start.6
  562.4 4.2 fusion.36
  566.6 5.8 all_gather.7
  572.4 0.7 fusion.20
  573.2 1.3 copy.10
  574.5 11.7 %broadcast_in_dim.58 = bf16[2048,8192]{1,0:T(8,128)(2,1)} broadcast(bf16[]{:T(256)} %constant.64.clone.1), dimensions={} | broadcast | bytes 33554432 | tf_op jit(solution)/shard_map/broadcast_in_dim | solution.py:13
  586.2 2.4 constant_dynamic-update-slice_fusion.7
  588.5 4.5 fusion.43
  593.0 17.8 %all-reduce.1 = bf16[1024,128]{0,1:T(8,128)(2,1)S(1)} all-reduce(f32[1024,128]{0,1:T(8,128)S(1)} %fusion.33), channel_id=1, replica_groups=mesh['trial'=8,'tensor'=4] {'tensor'}, use_global_device_ids=true, to_apply=%region_0.1 | all-reduce | flops 131072 | bytes 786432 | tf_op jit(solution)/shard_map/psum | solution.py:57
  610.9 4.6 constant_dynamic-update-slice_fusion.6
  615.4 4.6 constant_dynamic-update-slice_fusion.5
  620.0 4.6 constant_dynamic-update-slice_fusion.4
  624.5 4.6 constant_dynamic-update-slice_fusion.3
  629.1 4.6 constant_dynamic-update-slice_fusion.2
  633.7 4.6 constant_dynamic-update-slice_fusion.1
  638.3 15.2 %collective-permute-done.6 = bf16[2048,1024]{1,0:T(8,128)(2,1)} collective-permute-done((bf16[2048,1024]{1,0:T(8,128)(2,1)}, bf16[2048,1024]{1,0:T(8,128)(2,1)}, u32[]{:S(2)}, u32[]{:S(2)}) %collective-permute-start.6) | collective-permute-done | bytes 4194336 | tf_op jit(solution)/shard_map/ppermute | solution.py:18
  653.5 4.6 constant_dynamic-update-slice_fusion
  658.2 45.1 %fusion = bf16[1,1024,2048]{2,1,0:T(8,128)(2,1)} fusion(f32[1024,2048]{1,0:T(8,128)} %fusion.43, f32[]{:T(128)S(6)} %div.15, bf16[1024,8192]{1,0:T(8,128)(2,1)} %all-gather.2.cloned.1.call-done, bf16[2048,8192]{1,0:T(8,128)(2,1)} %constant_dynamic-update-slice_fusion), kind=kOutput, calls=%fused_computation.1 | convolution fusion | flops 34366029824 | bytes 62914564 | tf_op jit(solution)/shard_map/tk,hk->th/dot_general | solution.py:31
  703.3 3.9 fusion.26
  (14 shorter events, 0.1 us)
Async XLA Ops:
  7.2 651.0 %all-gather.2.cloned.1.call-start = ((), (), s32[]{:S(2)}) async-start(), calls=%async_computation | async-start | bytes 20971520 | tf_op jit(solution)/shard_map/all_gather | solution.py:60
  12.4 372.7 %copy-start.3 = (bf16[1,2048,128]{2,1,0:T(8,128)(2,1)S(1)}, bf16[1,2048,128]{2,1,0:T(8,128)(2,1)}, u32[]{:S(2)}) copy-start(bf16[1,2048,128]{2,1,0:T(8,128)(2,1)} %param.10) | copy-start | bytes 1572868
  12.4 183.0 %collective-permute-start = (bf16[2048,1024]{1,0:T(8,128)(2,1)}, bf16[2048,1024]{1,0:T(8,128)(2,1)S(1)}, u32[]{:S(2)}, u32[]{:S(2)}) collective-permute-start(bf16[2048,1024]{1,0:T(8,128)(2,1)} %param.9), channel_id=1, source_target_pairs={{0,4},{4,8},{8,12},{12,16},{16,20},{20,24},{24,28},{28,0},{1,5},{5... | collective-permute-start | bytes 12582920 | tf_op jit(solution)/shard_map/ppermute | solution.py:18
  15.5 184.4 %collective-permute-start.1 = (bf16[2048,1024]{1,0:T(8,128)(2,1)}, bf16[2048,1024]{1,0:T(8,128)(2,1)}, u32[]{:S(2)}, u32[]{:S(2)}) collective-permute-start(bf16[2048,1024]{1,0:T(8,128)(2,1)} %param.9), channel_id=1, source_target_pairs={{0,28},{4,0},{8,4},{12,8},{16,12},{20,16},{24,20},{28,24},{1,29},{... | collective-permute-start | bytes 12582920 | tf_op jit(solution)/shard_map/ppermute | solution.py:23
  195.5 2.0 copy-start.2
  197.5 181.2 %collective-permute-start.2 = (bf16[2048,1024]{1,0:T(8,128)(2,1)S(1)}, bf16[2048,1024]{1,0:T(8,128)(2,1)}, u32[]{:S(2)}, u32[]{:S(2)}) collective-permute-start(bf16[2048,1024]{1,0:T(8,128)(2,1)S(1)} %collective-permute-done), channel_id=1, source_target_pairs={{0,4},{4,8},{8,12},{12,16},{16,20},{20,24},{24,28},{28,0},{1,5},{5... | collective-permute-start | bytes 12582920 | tf_op jit(solution)/shard_map/ppermute | solution.py:18
  199.9 182.1 %collective-permute-start.3 = (bf16[2048,1024]{1,0:T(8,128)(2,1)}, bf16[2048,1024]{1,0:T(8,128)(2,1)}, u32[]{:S(2)}, u32[]{:S(2)}) collective-permute-start(bf16[2048,1024]{1,0:T(8,128)(2,1)} %collective-permute-done.1), channel_id=1, source_target_pairs={{0,28},{4,0},{8,4},{12,8},{16,12},{20,16},{24,20},{28,24},{1,29},{... | collective-permute-start | bytes 12582920 | tf_op jit(solution)/shard_map/ppermute | solution.py:23
  378.7 181.2 %collective-permute-start.4 = (bf16[2048,1024]{1,0:T(8,128)(2,1)}, bf16[2048,1024]{1,0:T(8,128)(2,1)}, u32[]{:S(2)}, u32[]{:S(2)}) collective-permute-start(bf16[2048,1024]{1,0:T(8,128)(2,1)} %collective-permute-done.2), channel_id=1, source_target_pairs={{0,4},{4,8},{8,12},{12,16},{16,20},{20,24},{24,28},{28,0},{1,5},{5... | collective-permute-start | bytes 12582920 | tf_op jit(solution)/shard_map/ppermute | solution.py:18
  382.0 251.7 %collective-permute-start.5 = (bf16[2048,1024]{1,0:T(8,128)(2,1)}, bf16[2048,1024]{1,0:T(8,128)(2,1)}, u32[]{:S(2)}, u32[]{:S(2)}) collective-permute-start(bf16[2048,1024]{1,0:T(8,128)(2,1)} %collective-permute-done.3), channel_id=1, source_target_pairs={{0,28},{4,0},{8,4},{12,8},{16,12},{20,16},{24,20},{28,24},{1,29},{... | collective-permute-start | bytes 12582920 | tf_op jit(solution)/shard_map/ppermute | solution.py:23
  388.8 183.6 %copy-start = (bf16[1,1024,2048]{2,1,0:T(8,128)(2,1)S(1)}, bf16[1,1024,2048]{2,1,0:T(8,128)(2,1)}, u32[]{:S(2)}) copy-start(bf16[1,1024,2048]{2,1,0:T(8,128)(2,1)} %param.7) | copy-start | bytes 12582916
  559.9 93.6 %collective-permute-start.6 = (bf16[2048,1024]{1,0:T(8,128)(2,1)}, bf16[2048,1024]{1,0:T(8,128)(2,1)}, u32[]{:S(2)}, u32[]{:S(2)}) collective-permute-start(bf16[2048,1024]{1,0:T(8,128)(2,1)} %collective-permute-done.4), channel_id=1, source_target_pairs={{0,4},{4,8},{8,12},{12,16},{16,20},{20,24},{24,28},{28,0},{1,5},{5... | collective-permute-start | bytes 12582920 | tf_op jit(solution)/shard_map/ppermute | solution.py:18
  574.5 11.7 %copy-start.1 = (bf16[2048,1024]{1,0:T(8,128)(2,1)S(1)}, bf16[2048,1024]{1,0:T(8,128)(2,1)}, u32[]{:S(2)}) copy-start(bf16[2048,1024]{1,0:T(8,128)(2,1)} %param.9) | copy-start | bytes 12582916
Sparse Core Ops, SparseCore 0:
  12.6 108.6 all-gather.1
